TPU v7x, 32 devices: a whole 2x2x4 slice. The times are simulated.
32 devices in a mesh: dp: 8 (over y, x, core), mp: 4 (over z).
Axes of the slice: x: 2, y: 2, z: 4, core: 2. Of those that a mesh axis runs over, the one named last changes fastest.
Arguments:
- hidden: bfloat16 [192, 256, 4096], P(('dp', 'mp')), may hold values from -6 to 6
- lengths: int32 [192], P(('dp', 'mp')), may hold values from 32 to 256, as said below
- list_ids: int32 [192], P('dp'), may hold values from 0 to 65535, as said below
- gain: bfloat16 [4096], replicated, may hold values from 0.099609375 to 1.8984375
- head: bfloat16 [4096, 1024], P('dp', 'mp'), may hold values from -0.09375 to 0.09375
- list_slot: int32 [65536], replicated, may hold values from 0 to 65535, as said below
- centroids: bfloat16 [65536, 1024], P('dp'), may hold values from -0.59765625 to 0.59765625
- rotation: bfloat16 [1024, 1024], P('mp'), may hold values from -0.1875 to 0.1875
Outputs:
- codes: bfloat16 [192, 1024], P('dp', 'mp')
- scales: bfloat16 [192, 16], P('dp', 'mp')
Inputs may be any that keep to these rules, and one draw needn't show every extreme that they name: `list_ids`: in each aligned block of 24 passages, at most 6 have lists in one range of 8192 lists (list id // 8192); one range holds exactly 6 of them in every block. Each list's row in the centroid table; list_slot[l] // 8192 equals l // 8192, and each row of a range once. `lengths`: some passage has exactly 256 valid tokens.
All inputs are finite; a program needn't handle non-finite values. Where the computation divides by a largest or mean magnitude, that divisor is 1e-20 or more.
Results may differ from a plain program's by a relative error of at most 0.013.
Values may be sent and summed in bfloat16 or wider, within the bound.
No kernel may reach another device: no remote copies, remote signals or barrier semaphores. Data moves between devices by JAX's collectives and lax.ppermute only.
A program may use at most 64 MiB of HBM per device.

v0:
```python
import jax
import jax.numpy as jnp
from jax import lax
from jax.sharding import PartitionSpec as P

BLOCK = 64


def quantize(rotated):
    lead = rotated.shape[:-1]
    width = rotated.shape[-1]
    blocks = rotated.reshape(lead + (width // BLOCK, BLOCK))
    scale = jnp.max(jnp.abs(blocks), axis=-1) + 1e-06
    codes = (blocks / scale[..., None]).reshape(lead + (width,)).astype(jnp.bfloat16)
    return (codes, scale.astype(jnp.bfloat16))


def pick_own(placing, buckets):
    picked = jnp.einsum("poc,oce->pe", placing, buckets, preferred_element_type=jnp.float32)
    return picked.astype(buckets.dtype)


def per_device(hidden, lengths, list_ids, gain, head, list_slot, centroids, rotation):
    passes, slots, width = hidden.shape
    states = hidden.astype(jnp.float32)
    mean_square = jnp.mean(states * states, axis=-1)
    valid = jnp.arange(slots, dtype=jnp.int32)[None, :] < lengths[:, None]
    weights = (
        jnp.where(valid, lax.rsqrt(mean_square + 1e-05), 0.0) / lengths.astype(jnp.float32)[:, None]
    )
    pooled_mine = (jnp.einsum("pl,pld->pd", weights, states) * gain.astype(jnp.float32)).astype(
        jnp.bfloat16
    )
    pooled = lax.all_gather(pooled_mine, "mp", axis=0, tiled=True)
    group = pooled.shape[0]
    col_width = head.shape[1]
    projected = jnp.dot(
        pooled, lax.all_gather(head, "dp", axis=0, tiled=True), preferred_element_type=jnp.float32
    ).astype(jnp.bfloat16)
    owners = lax.axis_size("dp")
    lists_own = centroids.shape[0]
    capacity = max(2, 2 * group // owners)
    col_start = lax.axis_index("mp") * col_width
    cent_cols = lax.dynamic_slice_in_dim(centroids, col_start, col_width, 1)
    owner = list_ids // lists_own
    local_row = list_slot[list_ids] % lists_own
    matches = (owner[:, None] == jnp.arange(owners, dtype=jnp.int32)[None, :]).astype(jnp.int32)
    earlier = jnp.cumsum(matches, axis=0) - matches
    rank = jnp.sum(earlier * matches, axis=1)
    placed = (matches[:, :, None] > 0) & (
        rank[:, None, None] == jnp.arange(capacity, dtype=jnp.int32)[None, None, :]
    )
    placing = placed.astype(jnp.bfloat16)
    bucket_ids = jnp.sum(jnp.where(placed, local_row[:, None, None], 0), axis=0)
    cents_back = lax.all_to_all(
        cent_cols[lax.all_to_all(bucket_ids, "dp", split_axis=0, concat_axis=0, tiled=True)],
        "dp",
        split_axis=0,
        concat_axis=0,
        tiled=True,
    )
    cents = pick_own(placing, cents_back)
    resid = (projected.astype(jnp.float32) - cents.astype(jnp.float32)).astype(jnp.bfloat16)
    partial_value = jnp.dot(resid, rotation, preferred_element_type=jnp.float32)
    rotated = lax.psum_scatter(partial_value, "mp", scatter_dimension=1, tiled=True)
    codes, scales = quantize(rotated)
    return (codes, scales)


def solution(mesh):
    in_specs = (
        P(("dp", "mp"), None, None),
        P(("dp", "mp")),
        P("dp"),
        P(),
        P("dp", "mp"),
        P(),
        P("dp", None),
        P("mp", None),
    )
    out_specs = (P("dp", "mp"), P("dp", "mp"))
    return jax.shard_map(
        per_device, mesh=mesh, in_specs=in_specs, out_specs=out_specs, check_vma=False
    )
```

profile of v0, /device:TPU:0, one launch (start us, length us, event | category | flops | bytes accessed | tf_op | source)
XLA Modules:
  0.0 92.6 jit_solution(1821076101298347327)
XLA Ops:
  7.2 0.7 and_select_fusion.2
  8.0 0.2 select_reduce_fusion
  8.3 1.7 %gather_fusion = s32[24]{0:T(128)S(1)} fusion(s32[65536]{0:T(1024)} %param.13, s32[1024]{0:T(1024)S(1)} %pad_clamp_fusion.1), kind=kCustom, calls=%fused_computation | custom fusion | bytes 288 | tf_op jit(solution)/shard_map/gather | solution.py:46
  10.0 0.8 fusion.10
  10.8 5.2 %all-to-all-start = ((s32[8,1,6]{2,1,0:T(1,128)}), s32[8,1,6]{2,1,0:T(1,128)S(1)}, u32[]{:S(2)}, u32[]{:S(2)}) async-start(s32[8,1,6]{2,1,0:T(1,128)} %bitcast.4), calls=%async_computation | async-start | bytes 8192 | tf_op jit(solution)/shard_map/all_to_all | solution.py:56
  16.1 0.7 all-gather.3.cloned.1.call-update
  16.7 7.1 %multiply_reduce_fusion = f32[6,256]{1,0:T(8,128)S(1)} fusion(bf16[6,256,4096]{2,1,0:T(8,128)(2,1)} %param.8), kind=kLoop, calls=%fused_computation.2 | loop fusion | flops 18872832 | bytes 12589056 | tf_op jit(solution)/shard_map/reduce_sum | solution.py:26
  23.9 6.5 %fusion.17 = f32[6,1,4096]{2,1,0:T(1,128)S(1)} fusion(bf16[6,256,4096]{2,1,0:T(8,128)(2,1)} %param.8, bf16[6,256,1]{1,0,2:T(8,128)(2,1)S(1)} %divide_bitcast_fusion), kind=kOutput, calls=%fused_computation.27 | convolution fusion | flops 12582912 | bytes 12684288 | tf_op jit(solution)/shard_map/pl,pld->pd/dot_general | solution.py:31
  30.5 4.4 %constant_dynamic-slice_fusion = bf16[8192,256]{1,0:T(8,128)(2,1)} fusion(bf16[8192,1024]{1,0:T(8,128)(2,1)} %param.14, s32[]{:T(128)S(6)} %select_n.42), kind=kLoop, calls=%fused_computation.42 | loop fusion | bytes 8388612 | tf_op jit(solution)/shard_map/dynamic_slice | solution.py:44
  34.9 14.2 %all-gather = bf16[4,6,4096]{2,1,0:T(8,128)(2,1)S(1)} all-gather(bf16[1,6,4096]{2,1,0:T(8,128)(2,1)S(1)} %fusion.7), channel_id=1, replica_groups=mesh['dp'=8,'mp'=4] {'mp'}, dimensions={0}, use_global_device_ids=true | all-gather | bytes 245760 | tf_op jit(solution)/shard_map/all_gather | solution.py:34
  49.3 0.1 copy.19
  49.5 3.4 %gather_fusion.1 = bf16[48,256]{1,0:T(8,128)(2,1)S(1)} fusion(bf16[8192,256]{1,0:T(8,128)(2,1)} %constant_dynamic-slice_fusion, s32[1024]{0:T(1024)S(1)} %pad_clamp_fusion), kind=kCustom, calls=%fused_computation.1 | custom fusion | bytes 49344 | tf_op jit(solution)/shard_map/gather | solution.py:56
  52.9 0.6 reshape.111
  53.5 4.0 %all-to-all-start.1 = ((bf16[8,6,256]{2,1,0:T(8,128)(2,1)}), bf16[8,6,256]{2,1,0:T(8,128)(2,1)S(1)}, u32[]{:S(2)}, u32[]{:S(2)}) async-start(bf16[8,6,256]{2,1,0:T(8,128)(2,1)} %reshape.111), calls=%async_computation.1 | async-start | bytes 65536 | tf_op jit(solution)/shard_map/all_to_all | solution.py:55
  57.5 2.0 %fusion.4 = f32[24,256]{1,0:T(8,128)S(1)} fusion(bf16[24,4096]{1,0:T(8,128)(2,1)S(1)} %reshape.121, bf16[4096,256]{1,0:T(8,128)(2,1)} %all-gather.3.cloned.1.call-done), kind=kOutput, calls=%fused_computation.9 | convolution fusion | flops 50343936 | bytes 2318336 | tf_op jit(solution)/shard_map/dot_general | solution.py:37
  59.5 2.8 %all-to-all-done.1 = bf16[8,6,256]{2,1,0:T(8,128)(2,1)S(1)} async-done(((bf16[8,6,256]{2,1,0:T(8,128)(2,1)}), bf16[8,6,256]{2,1,0:T(8,128)(2,1)S(1)}, u32[]{:S(2)}, u32[]{:S(2)}) %all-to-all-start.1) | async-done | bytes 24608 | tf_op jit(solution)/shard_map/all_to_all | solution.py:55
  62.3 1.0 %fusion.5 = f32[24,1024]{1,0:T(8,128)} fusion(bf16[256,1024]{1,0:T(8,128)(2,1)S(1)} %copy-done, f32[24,256]{1,0:T(8,128)S(1)} %fusion.4, bf16[8,6,256]{2,1,0:T(8,128)(2,1)S(1)} %all-to-all-done.1, pred[24,6]{0,1:T(8,128)(4,1)S(1)} %iota_compare_fusion.2, pred[24,8]{0,1:T(8,128)(4,1)S(1)} %copy.16), kind=kOutput, calls=%fused_computation.10 | convolution fusion | flops 13198464 | bytes 672080 | tf_op jit(solution)/shard_map/dot_general | solution.py:64
  63.3 19.3 %reduce-scatter.2.cloned.1.call-done = f32[24,256]{1,0:T(8,128)} async-done(((f32[24,1024]{1,0:T(8,128)}), f32[24,256]{1,0:T(8,128)}) %reduce-scatter.2.cloned.1.call-update) | async-done | bytes 24592 | tf_op jit(solution)/shard_map/reduce_scatter | solution.py:65
  82.6 0.7 abs.6
  83.3 0.1 abs.7
  83.4 0.1 reduce_max.9
  83.6 0.1 div.46
  83.7 0.7 copy.20
  84.4 1.3 %divide_convert_fusion = bf16[24,256]{1,0:T(8,128)(2,1)} fusion(f32[24,256]{1,0:T(8,128)} %reduce-scatter.2.cloned.1.call-done, f32[24,256]{1,0:T(8,128)S(1)} %div.46), kind=kLoop, calls=%fused_computation.17 | loop fusion | flops 12288 | bytes 61440 | tf_op jit(solution)/shard_map/convert_element_type | solution.py:14
  (28 shorter events, 0.8 us)
Async XLA Ops:
  7.2 55.2 %copy-start = (bf16[256,1024]{1,0:T(8,128)(2,1)S(1)}, bf16[256,1024]{1,0:T(8,128)(2,1)}, u32[]{:S(2)}) copy-start(bf16[256,1024]{1,0:T(8,128)(2,1)} %param.15) | copy-start | bytes 1572868
  7.2 16.6 %copy-start.2 = (s32[6]{0:T(128)S(1)}, s32[6]{0:T(128)}, u32[]{:S(2)}) copy-start(s32[6]{0:T(128)} %param.9) | copy-start | bytes 76
  7.2 16.6 %copy-start.1 = (bf16[4096]{0:T(1024)(128)(2,1)S(1)}, bf16[4096]{0:T(1024)(128)(2,1)}, u32[]{:S(2)}) copy-start(bf16[4096]{0:T(1024)(128)(2,1)} %param.11) | copy-start | bytes 24580
  10.8 38.4 %all-to-all-start = ((s32[8,1,6]{2,1,0:T(1,128)}), s32[8,1,6]{2,1,0:T(1,128)S(1)}, u32[]{:S(2)}, u32[]{:S(2)}) async-start(s32[8,1,6]{2,1,0:T(1,128)} %bitcast.4), calls=%async_computation | async-start | bytes 8192 | tf_op jit(solution)/shard_map/all_to_all | solution.py:56
  16.0 41.5 %all-gather.3.cloned.1.call-start = ((), (), s32[]{:S(2)}) async-start(), calls=%async_computation.3 | async-start | bytes 2359296 | tf_op jit(solution)/shard_map/all_gather | solution.py:38
  53.5 8.8 %all-to-all-start.1 = ((bf16[8,6,256]{2,1,0:T(8,128)(2,1)}), bf16[8,6,256]{2,1,0:T(8,128)(2,1)S(1)}, u32[]{:S(2)}, u32[]{:S(2)}) async-start(bf16[8,6,256]{2,1,0:T(8,128)(2,1)} %reshape.111), calls=%async_computation.1 | async-start | bytes 65536 | tf_op jit(solution)/shard_map/all_to_all | solution.py:55
  57.5 25.1 %reduce-scatter.2.cloned.1.call-start = ((), (), s32[]{:S(2)}) async-start(), calls=%async_computation.4 | async-start | bytes 122880 | tf_op jit(solution)/shard_map/reduce_scatter | solution.py:65
Sparse Core Ops, SparseCore 0:
  18.7 29.4 all-gather.2
  63.4 19.0 reduce-scatter.1
where the time goes:
time: 93.2 us; the launch traced here: 92.6 us
  waiting for transfers between devices  22.8 us (24%)
  blocking collectives  14.2 us (15%)
  between operations  14.2 us (15%)
  local copies, waits for them, and re-layouts  11.4 us (12%)
  other arithmetic  11.3 us (12%)
  matrix products  9.46 us (10%)
  starting transfers between devices  9.28 us (10%)
    reduce_scatter x1, waiting for transfers between devices, per_device(): lax.psum_scatter(partial_value, 'mp', scatter_dimension=1, tiled=True)  19.3 us
    all_gather x1, blocking collectives, per_device(): pooled = lax.all_gather(pooled_mine, 'mp', axis=0, tiled=True)  14.2 us
    reduce_sum x1, other arithmetic, per_device(): mean_square = jnp.mean(states * states, axis=-1)  7.07 us
    dot_general x1, matrix products, per_device(): jnp.einsum('pl,pld->pd', weights, states) * gain.astype(jnp.float32)  6.5 us
    all_to_all x1, starting transfers between devices, per_device(): lax.all_to_all(bucket_ids, 'dp', split_axis=0, concat_axis=0, tiled=True)  5.2 us
    dynamic_slice x1, local copies, waits for them, and re-layouts, per_device(): cent_cols = lax.dynamic_slice_in_dim(centroids, col_start, col_width, 1)  4.4 us
    all_to_all x1, starting transfers between devices, per_device(): lax.all_to_all(cent_cols[lax.all_to_all(bucket_ids, 'dp', split_axis=0, c...  4.01 us
    gather x2, local copies, waits for them, and re-layouts, per_device(): cent_cols[lax.all_to_all(bucket_ids, 'dp', split_axis=0, concat_axis=0, t...  3.97 us
  transfers between devices with their start and end apart: 4, of which 2 were waited for; matrix products, arithmetic and copies ran while one was open for 26% of the time, Pallas kernels for 0%

commit v1 on v0

--- a/solution.py
+++ b/solution.py
@@ -31,7 +31,27 @@
     pooled_mine = (jnp.einsum("pl,pld->pd", weights, states) * gain.astype(jnp.float32)).astype(
         jnp.bfloat16
     )
-    pooled = lax.all_gather(pooled_mine, "mp", axis=0, tiled=True)
+    n_lanes = lax.axis_size("mp")
+    chunks = []
+    num = 0
+    while num < n_lanes:
+        chunks.append((num, (num + 1) % n_lanes))
+        num += 1
+    copies = []
+    num = 0
+    while num < n_lanes:
+        copies.append((num, (num - 1) % n_lanes))
+        num += 1
+    carry_out, fresh = ([pooled_mine], [pooled_mine])
+    for _ in range(n_lanes // 2):
+        carry_out.append(lax.ppermute(carry_out[-1], axis_name="mp", perm=chunks))
+    dev = 0
+    while dev < (n_lanes - 1) // 2:
+        state_next = lax.ppermute(fresh[-1], axis_name="mp", perm=copies)
+        fresh.append(state_next)
+        dev += 1
+    row_out = jnp.concatenate([*carry_out[::-1], *fresh[1:]], 0)
+    pooled = jnp.roll(row_out, (lax.axis_index("mp") - n_lanes // 2) * pooled_mine.shape[0], 0)
     group = pooled.shape[0]
     col_width = head.shape[1]
     projected = jnp.dot(

time: 93.2 us -> 86.6 us (0.929)
  blocking collectives: 14.2 us -> 0 us
  starting transfers between devices: 9.28 us -> 13.4 us
  waiting for transfers between devices: 22.8 us -> 25.5 us
    all_gather x1 -> x0, blocking collectives: 14.2 us -> none  [per_device(): pooled = lax.all_gather(pooled_mine, 'mp', axis=0, tiled=True)]
    ppermute x0 -> x3, starting transfers between devices: none -> 3.84 us  [the longest x1 2.22 us: per_device(): state_next = lax.ppermute(fresh[-1], axis_name='mp', perm=copies)]
    ppermute x0 -> x3, waiting for transfers between devices: none -> 3.29 us  [the longest x2 3.29 us: per_device(): carry_out.append(lax.ppermute(carry_out[-1], axis_name='mp', perm=chunks))]
    dot_general x1, matrix products: 0.98 us -> 2.92 us  [per_device(): partial_value = jnp.dot(resid, rotation, preferred_element_type=jnp.float32)]
    dot_general x1, matrix products: 1.98 us -> 0.2 us  [pick_own(): jnp.einsum('poc,oce->pe', placing, buckets, preferred_element_type=jnp.fl...]
  transfers between devices with their start and end apart: 4 -> 7, of which waited for: 2 -> 3; matrix products, arithmetic and copies ran while one was open for 26% -> 27% of each run, Pallas kernels for 0% -> 0%
where the time goes in v1:
time: 86.6 us; the launch traced here: 86.1 us
  waiting for transfers between devices  25.5 us (29%)
  between operations  14.2 us (16%)
  starting transfers between devices  13.4 us (15%)
  local copies, waits for them, and re-layouts  12.1 us (14%)
  other arithmetic  11.3 us (13%)
  matrix products  9.62 us (11%)
    reduce_scatter x1, waiting for transfers between devices, per_device(): lax.psum_scatter(partial_value, 'mp', scatter_dimension=1, tiled=True)  18.9 us
    reduce_sum x1, other arithmetic, per_device(): mean_square = jnp.mean(states * states, axis=-1)  7.07 us
    dot_general x1, matrix products, per_device(): jnp.einsum('pl,pld->pd', weights, states) * gain.astype(jnp.float32)  6.5 us
    all_to_all x1, starting transfers between devices, per_device(): lax.all_to_all(bucket_ids, 'dp', split_axis=0, concat_axis=0, tiled=True)  5.2 us
    dynamic_slice x1, local copies, waits for them, and re-layouts, per_device(): cent_cols = lax.dynamic_slice_in_dim(centroids, col_start, col_width, 1)  4.4 us
    all_to_all x1, starting transfers between devices, per_device(): lax.all_to_all(cent_cols[lax.all_to_all(bucket_ids, 'dp', split_axis=0, c...  4.28 us
    gather x2, local copies, waits for them, and re-layouts, per_device(): cent_cols[lax.all_to_all(bucket_ids, 'dp', split_axis=0, concat_axis=0, t...  3.97 us
    ppermute x2, waiting for transfers between devices, per_device(): carry_out.append(lax.ppermute(carry_out[-1], axis_name='mp', perm=chunks))  3.29 us
  transfers between devices with their start and end apart: 7, of which 3 were waited for; matrix products, arithmetic and copies ran while one was open for 27% of the time, Pallas kernels for 0%

profile of v1, /device:TPU:0, one launch (start us, length us, event | category | flops | bytes accessed | tf_op | source)
XLA Modules:
  0.0 86.1 jit_solution(13283783007853853963)
XLA Ops:
  7.2 0.7 and_select_fusion.2
  8.0 0.2 select_reduce_fusion
  8.3 1.7 %gather_fusion = s32[24]{0:T(128)S(1)} fusion(s32[65536]{0:T(1024)} %param.13, s32[1024]{0:T(1024)S(1)} %pad_clamp_fusion.1), kind=kCustom, calls=%fused_computation | custom fusion | bytes 288 | tf_op jit(solution)/shard_map/gather | solution.py:66
  10.0 0.8 fusion.10
  10.8 5.2 %all-to-all-start = ((s32[8,1,6]{2,1,0:T(1,128)}), s32[8,1,6]{2,1,0:T(1,128)S(1)}, u32[]{:S(2)}, u32[]{:S(2)}) async-start(s32[8,1,6]{2,1,0:T(1,128)} %bitcast.3), calls=%async_computation | async-start | bytes 8192 | tf_op jit(solution)/shard_map/all_to_all | solution.py:76
  16.1 0.7 all-gather.2.cloned.1.call-update
  16.7 7.1 %multiply_reduce_fusion = f32[6,256]{1,0:T(8,128)S(1)} fusion(bf16[6,256,4096]{2,1,0:T(8,128)(2,1)} %param.8), kind=kLoop, calls=%fused_computation.2 | loop fusion | flops 18872832 | bytes 12589056 | tf_op jit(solution)/shard_map/reduce_sum | solution.py:26
  23.9 6.5 %fusion.15 = f32[6,1,4096]{2,1,0:T(1,128)S(1)} fusion(bf16[6,256,4096]{2,1,0:T(8,128)(2,1)} %param.8, bf16[6,256,1]{1,0,2:T(8,128)(2,1)S(1)} %divide_bitcast_fusion), kind=kOutput, calls=%fused_computation.27 | convolution fusion | flops 12582912 | bytes 12684288 | tf_op jit(solution)/shard_map/pl,pld->pd/dot_general | solution.py:31
  30.5 1.6 %collective-permute-start = (bf16[6,4096]{1,0:T(8,128)(2,1)S(1)}, bf16[6,4096]{1,0:T(8,128)(2,1)S(1)}, u32[]{:S(2)}, u32[]{:S(2)}) collective-permute-start(bf16[6,4096]{1,0:T(8,128)(2,1)S(1)} %fusion.8), channel_id=1, source_target_pairs={{0,1},{1,2},{2,3},{3,0},{4,5},{5,6},{6,7},{7,4},{8,9},{9,10},{10,1... | collective-permute-start | bytes 147464 | tf_op jit(solution)/shard_map/ppermute | solution.py:47
  32.1 4.4 %constant_dynamic-slice_fusion = bf16[8192,256]{1,0:T(8,128)(2,1)} fusion(bf16[8192,1024]{1,0:T(8,128)(2,1)} %param.14, s32[]{:T(128)S(6)} %select_n.56), kind=kLoop, calls=%fused_computation.42 | loop fusion | bytes 8388612 | tf_op jit(solution)/shard_map/dynamic_slice | solution.py:64
  36.8 3.4 %gather_fusion.1 = bf16[48,256]{1,0:T(8,128)(2,1)S(1)} fusion(bf16[8192,256]{1,0:T(8,128)(2,1)} %constant_dynamic-slice_fusion, s32[1024]{0:T(1024)S(1)} %pad_clamp_fusion), kind=kCustom, calls=%fused_computation.1 | custom fusion | bytes 49344 | tf_op jit(solution)/shard_map/gather | solution.py:76
  40.1 0.6 reshape.111
  40.8 4.3 %all-to-all-start.1 = ((bf16[8,6,256]{2,1,0:T(8,128)(2,1)}), bf16[8,6,256]{2,1,0:T(8,128)(2,1)S(1)}, u32[]{:S(2)}, u32[]{:S(2)}) async-start(bf16[8,6,256]{2,1,0:T(8,128)(2,1)} %reshape.111), calls=%async_computation.1 | async-start | bytes 65536 | tf_op jit(solution)/shard_map/all_to_all | solution.py:75
  45.1 2.2 %collective-permute-start.2 = (bf16[6,4096]{1,0:T(8,128)(2,1)S(1)}, bf16[6,4096]{1,0:T(8,128)(2,1)S(1)}, u32[]{:S(2)}, u32[]{:S(2)}) collective-permute-start(bf16[6,4096]{1,0:T(8,128)(2,1)S(1)} %fusion.8), channel_id=1, source_target_pairs={{0,3},{1,0},{2,1},{3,2},{4,7},{5,4},{6,5},{7,6},{8,11},{9,8},{10,9... | collective-permute-start | bytes 147464 | tf_op jit(solution)/shard_map/ppermute | solution.py:50
  47.3 2.6 %all-to-all-done.1 = bf16[8,6,256]{2,1,0:T(8,128)(2,1)S(1)} async-done(((bf16[8,6,256]{2,1,0:T(8,128)(2,1)}), bf16[8,6,256]{2,1,0:T(8,128)(2,1)S(1)}, u32[]{:S(2)}, u32[]{:S(2)}) %all-to-all-start.1) | async-done | bytes 24608 | tf_op jit(solution)/shard_map/all_to_all | solution.py:75
  49.9 0.2 fusion.1
  50.1 3.3 %collective-permute-done.1 = bf16[6,4096]{1,0:T(8,128)(2,1)S(1)} collective-permute-done((bf16[6,4096]{1,0:T(8,128)(2,1)S(1)}, bf16[6,4096]{1,0:T(8,128)(2,1)S(1)}, u32[]{:S(2)}, u32[]{:S(2)}) %collective-permute-start.1) | collective-permute-done | bytes 49184 | tf_op jit(solution)/shard_map/ppermute | solution.py:47
  53.4 0.8 concatenate.6
  54.3 2.9 %fusion.5 = f32[24,1024]{1,0:T(8,128)} fusion(bf16[256,1024]{1,0:T(8,128)(2,1)S(1)} %copy-done, f32[24,256]{1,0:T(8,128)S(1)} %fusion.1, bf16[4096,256]{1,0:T(8,128)(2,1)} %all-gather.2.cloned.1.call-done, bf16[48,4096]{1,0:T(8,128)(2,1)S(1)} %concatenate.6, s32[]{:T(128)S(6)} %select_n.54), kind=kOutput, calls=%fused_computation.10 | convolution fusion | flops 62939136 | bytes 2940932 | tf_op jit(solution)/shard_map/dot_general | solution.py:84
  57.2 18.9 %reduce-scatter.2.cloned.1.call-done = f32[24,256]{1,0:T(8,128)} async-done(((f32[24,1024]{1,0:T(8,128)}), f32[24,256]{1,0:T(8,128)}) %reduce-scatter.2.cloned.1.call-update) | async-done | bytes 24592 | tf_op jit(solution)/shard_map/reduce_scatter | solution.py:85
  76.1 0.7 abs.6
  77.1 0.1 div.46
  77.2 0.7 copy.20
  77.9 1.3 %divide_convert_fusion = bf16[24,256]{1,0:T(8,128)(2,1)} fusion(f32[24,256]{1,0:T(8,128)} %reduce-scatter.2.cloned.1.call-done, f32[24,256]{1,0:T(8,128)S(1)} %div.46), kind=kLoop, calls=%fused_computation.17 | loop fusion | flops 12288 | bytes 61440 | tf_op jit(solution)/shard_map/convert_element_type | solution.py:14
  (33 shorter events, 1.1 us)
Async XLA Ops:
  7.2 47.1 %copy-start = (bf16[256,1024]{1,0:T(8,128)(2,1)S(1)}, bf16[256,1024]{1,0:T(8,128)(2,1)}, u32[]{:S(2)}) copy-start(bf16[256,1024]{1,0:T(8,128)(2,1)} %param.15) | copy-start | bytes 1572868
  7.2 16.6 %copy-start.2 = (s32[6]{0:T(128)S(1)}, s32[6]{0:T(128)}, u32[]{:S(2)}) copy-start(s32[6]{0:T(128)} %param.9) | copy-start | bytes 76
  7.2 16.6 %copy-start.1 = (bf16[4096]{0:T(1024)(128)(2,1)S(1)}, bf16[4096]{0:T(1024)(128)(2,1)}, u32[]{:S(2)}) copy-start(bf16[4096]{0:T(1024)(128)(2,1)} %param.11) | copy-start | bytes 24580
  10.8 25.7 %all-to-all-start = ((s32[8,1,6]{2,1,0:T(1,128)}), s32[8,1,6]{2,1,0:T(1,128)S(1)}, u32[]{:S(2)}, u32[]{:S(2)}) async-start(s32[8,1,6]{2,1,0:T(1,128)} %bitcast.3), calls=%async_computation | async-start | bytes 8192 | tf_op jit(solution)/shard_map/all_to_all | solution.py:76
  16.0 38.2 %all-gather.2.cloned.1.call-start = ((), (), s32[]{:S(2)}) async-start(), calls=%async_computation.3 | async-start | bytes 2359296 | tf_op jit(solution)/shard_map/all_gather | solution.py:58
  30.5 16.8 %collective-permute-start = (bf16[6,4096]{1,0:T(8,128)(2,1)S(1)}, bf16[6,4096]{1,0:T(8,128)(2,1)S(1)}, u32[]{:S(2)}, u32[]{:S(2)}) collective-permute-start(bf16[6,4096]{1,0:T(8,128)(2,1)S(1)} %fusion.8), channel_id=1, source_target_pairs={{0,1},{1,2},{2,3},{3,0},{4,5},{5,6},{6,7},{7,4},{8,9},{9,10},{10,1... | collective-permute-start | bytes 147464 | tf_op jit(solution)/shard_map/ppermute | solution.py:47
  40.8 9.1 %all-to-all-start.1 = ((bf16[8,6,256]{2,1,0:T(8,128)(2,1)}), bf16[8,6,256]{2,1,0:T(8,128)(2,1)S(1)}, u32[]{:S(2)}, u32[]{:S(2)}) async-start(bf16[8,6,256]{2,1,0:T(8,128)(2,1)} %reshape.111), calls=%async_computation.1 | async-start | bytes 65536 | tf_op jit(solution)/shard_map/all_to_all | solution.py:75
  45.0 31.0 %reduce-scatter.2.cloned.1.call-start = ((), (), s32[]{:S(2)}) async-start(), calls=%async_computation.4 | async-start | bytes 122880 | tf_op jit(solution)/shard_map/reduce_scatter | solution.py:85
  45.1 5.0 %collective-permute-start.2 = (bf16[6,4096]{1,0:T(8,128)(2,1)S(1)}, bf16[6,4096]{1,0:T(8,128)(2,1)S(1)}, u32[]{:S(2)}, u32[]{:S(2)}) collective-permute-start(bf16[6,4096]{1,0:T(8,128)(2,1)S(1)} %fusion.8), channel_id=1, source_target_pairs={{0,3},{1,0},{2,1},{3,2},{4,7},{5,4},{6,5},{7,6},{8,11},{9,8},{10,9... | collective-permute-start | bytes 147464 | tf_op jit(solution)/shard_map/ppermute | solution.py:50
  47.3 6.1 %collective-permute-start.1 = (bf16[6,4096]{1,0:T(8,128)(2,1)S(1)}, bf16[6,4096]{1,0:T(8,128)(2,1)S(1)}, u32[]{:S(2)}, u32[]{:S(2)}) collective-permute-start(bf16[6,4096]{1,0:T(8,128)(2,1)S(1)} %collective-permute-done), channel_id=1, source_target_pairs={{0,1},{1,2},{2,3},{3,0},{4,5},{5,6},{6,7},{7,4},{8,9},{9,10},{10,1... | collective-permute-start | bytes 147464 | tf_op jit(solution)/shard_map/ppermute | solution.py:47
Sparse Core Ops, SparseCore 0:
  18.7 29.4 all-gather.1
  57.3 18.7 reduce-scatter.1
